TPU v7x, 512 devices: a whole 4x4x16 slice. The times are simulated.
512 devices in a mesh: group: 8 (over z_lo), shard: 64 (over z_hi, x, y, core).
Axes of the slice: x: 4, y: 4, z: 16 (z_hi: 2, z_lo: 8; z = z_hi * 8 + z_lo), core: 2. Of those that a mesh axis runs over, the one named last changes fastest.
Arguments:
- inner_embed: float32 [8, 15360, 768], P('group', 'shard'), may hold values from -6 to 6
- outer_embed: float32 [15360, 768], P('shard'), may hold values from -6 to 6
- moment_embed: float32 [15360, 768], P('shard'), may hold values from -6 to 6
- basis: float32 [15360, 64], P('shard'), may hold values from -6 to 6
- inner_attn: float32 [8, 768, 3072], P('group', 'shard'), may hold values from -6 to 6
- outer_attn: float32 [768, 3072], P(None, 'shard'), may hold values from -6 to 6
- moment_attn: float32 [768, 3072], P(None, 'shard'), may hold values from -6 to 6
- inner_norms: float32 [8, 4, 768], P('group', None, 'shard'), may hold values from -6 to 6
- outer_norms: float32 [4, 768], P(None, 'shard'), may hold values from -6 to 6
- moment_norms: float32 [4, 768], P(None, 'shard'), may hold values from -6 to 6
Outputs:
- new_embed: float32 [15360, 768], P('shard')
- new_moment_embed: float32 [15360, 768], P('shard')
- new_attn: float32 [768, 3072], P(None, 'shard')
- new_moment_attn: float32 [768, 3072], P(None, 'shard')
- new_norms: float32 [4, 768], P(None, 'shard')
- new_moment_norms: float32 [4, 768], P(None, 'shard')
- replica_attn: bfloat16 [768, 3072], P('shard')
All inputs are finite; a program needn't handle non-finite values.
Results may differ from a plain program's by a relative error of at most 0.0004.
Values may be sent and summed in bfloat16 or wider, within the bound.
A program may use at most 64 MiB of HBM per device.

v0:
```python
import math
import jax
import jax.numpy as jnp
from jax import lax
from jax.sharding import PartitionSpec as P

VOCAB = 15360
RANK = 64


def nesterov(outer, moment, delta):
    moment_new = 0.5 * moment + delta
    return (outer - (delta + 0.5 * moment_new), moment_new)


def on_device(
    inner_embed,
    outer_embed,
    moment_embed,
    basis,
    inner_attn,
    outer_attn,
    moment_attn,
    inner_norms,
    outer_norms,
    moment_norms,
):
    groups = lax.axis_size("group")
    embed_diff = outer_embed - inner_embed[0]
    partial_coeff = lax.dot_general(
        basis,
        embed_diff,
        (((0,), (0,)), ((), ())),
        precision=lax.Precision.HIGHEST,
        preferred_element_type=jnp.float32,
    )
    norm_diff = outer_norms - inner_norms[0]
    moved = lax.all_to_all(inner_attn[0], "shard", split_axis=1, concat_axis=0, tiled=True)
    attn_term = outer_attn - moved
    coeff_sum = lax.psum(partial_coeff, ("group", "shard"))
    attn_sum, norm_sum = lax.psum((attn_term, norm_diff), "group")
    attn_delta = attn_sum / groups
    norm_delta = norm_sum / groups
    coefficient = coeff_sum / groups
    embed_delta = jnp.dot(
        basis, coefficient, precision=lax.Precision.HIGHEST, preferred_element_type=jnp.float32
    ) * (1.0 / math.sqrt(RANK * VOCAB))
    new_embed, new_moment_embed = nesterov(outer_embed, moment_embed, embed_delta)
    new_attn, new_moment_attn = nesterov(outer_attn, moment_attn, attn_delta)
    new_norms, new_moment_norms = nesterov(outer_norms, moment_norms, norm_delta)
    replica_attn = lax.all_to_all(
        new_attn.astype(jnp.bfloat16), "shard", split_axis=0, concat_axis=1, tiled=True
    )
    return (
        new_embed,
        new_moment_embed,
        new_attn,
        new_moment_attn,
        new_norms,
        new_moment_norms,
        replica_attn,
    )


def solution(mesh):
    placed = (
        P("group", "shard", None),
        P("shard", None),
        P("shard", None),
        P("shard", None),
        P("group", "shard", None),
        P(None, "shard"),
        P(None, "shard"),
        P("group", None, "shard"),
        P(None, "shard"),
        P(None, "shard"),
    )
    return jax.shard_map(
        on_device,
        mesh=mesh,
        in_specs=placed,
        out_specs=(
            P("shard", None),
            P("shard", None),
            P(None, "shard"),
            P(None, "shard"),
            P(None, "shard"),
            P(None, "shard"),
            P("shard", None),
        ),
        check_vma=False,
    )
```

profile of v0, /device:TPU:1, one launch (start us, length us, event | category | flops | bytes accessed | tf_op | source)
XLA Modules:
  0.0 638.4 jit_solution(14730503204910227283)
XLA Ops:
  7.2 1.3 reduce
  8.5 0.2 all_to_all.28
  8.7 0.2 copy.34
  8.9 1.0 reshape.22
  9.9 22.4 %all-to-all-start = ((f32[64,1,576]{2,1,0:T(1,128)}), f32[64,1,576]{2,1,0:T(1,128)S(1)}, u32[]{:S(2)}, u32[]{:S(2)}) async-start(f32[64,1,576]{2,1,0:T(1,128)} %reshape.22), calls=%async_computation | async-start | bytes 327680 | tf_op jit(solution)/shard_map/all_to_all | solution.py:38
  32.4 0.2 copy.29
  32.6 17.3 %all-to-all-done = f32[64,1,576]{2,1,0:T(1,128)S(1)} async-done(((f32[64,1,576]{2,1,0:T(1,128)}), f32[64,1,576]{2,1,0:T(1,128)S(1)}, u32[]{:S(2)}, u32[]{:S(2)}) %all-to-all-start) | async-done | bytes 147488 | tf_op jit(solution)/shard_map/all_to_all | solution.py:38
  49.9 0.5 broadcast.29
  50.4 1.0 reduce.1
  51.4 0.2 reshape.23
  51.7 0.8 sub.20
  52.5 0.0 all-reduce.3.cloned.1.call-start
  52.6 0.4 copy-done.1
  53.0 0.2 copy-done.2
  53.2 1.3 convolution_bitcast_fusion
  54.5 0.9 copy-done.5
  55.4 0.2 copy.28
  55.5 0.5 copy-done.6
  56.1 27.7 %psum.23 = f32[4,12]{1,0:T(4,128)S(1)} all-reduce(f32[4,12]{1,0:T(4,128)S(1)} %bitcast_subtract_fusion.2), channel_id=1, replica_groups=mesh['group'=8,'shard'=64] {'group'}, use_global_device_ids=true, to_apply=%region_2.0 | all-reduce | flops 48 | bytes 384 | tf_op jit(solution)/shard_map/psum | solution.py:41
  83.8 0.6 add_subtract_fusion.2
  84.4 80.6 %all-reduce.5.cloned.1.call-done = f32[768,48]{1,0:T(8,128)} async-done(((f32[768,48]{1,0:T(8,128)}), f32[768,48]{1,0:T(8,128)}) %all-reduce.5.cloned.1.call-update) | async-done | bytes 147472 | tf_op jit(solution)/shard_map/psum | solution.py:41
  165.0 1.1 fusion.4
  166.1 0.1 all_to_all.32
  166.2 0.9 reshape.24
  167.1 16.1 %all-to-all-start.1 = ((bf16[64,2,288]{2,1,0:T(2,128)(2,1)}), bf16[64,2,288]{2,1,0:T(2,128)(2,1)S(1)}, u32[]{:S(2)}, u32[]{:S(2)}) async-start(bf16[64,2,288]{2,1,0:T(2,128)(2,1)} %reshape.24), calls=%async_computation.1 | async-start | bytes 196608 | tf_op jit(solution)/shard_map/all_to_all | solution.py:51
  183.3 442.5 %all-reduce.3.cloned.1.call-done = f32[64,768]{1,0:T(8,128)} async-done(((f32[64,768]{1,0:T(8,128)}), f32[64,768]{1,0:T(8,128)}) %all-reduce.3.cloned.1.call-update) | async-done | bytes 196624 | tf_op jit(solution)/shard_map/psum | solution.py:40
  625.8 2.9 add_subtract_fusion
  628.7 0.8 copy.31
  629.5 0.8 copy.32
  630.3 0.2 reshape.25
  630.6 0.1 copy.30
  630.6 0.9 all_to_all.35
  (21 shorter events, 0.2 us)
Async XLA Ops:
  7.2 45.4 %copy-start = (f32[240,64]{0,1:T(8,128)S(1)}, f32[240,64]{0,1:T(8,128)}, u32[]{:S(2)}) copy-start(f32[240,64]{0,1:T(8,128)} %param.13) | copy-start | bytes 184324
  9.9 22.4 %copy-start.4 = (f32[768,48]{0,1:T(8,128)S(1)}, f32[768,48]{0,1:T(8,128)}, u32[]{:S(2)}) copy-start(f32[768,48]{0,1:T(8,128)} %param.15) | copy-start | bytes 442372
  9.9 39.9 %all-to-all-start = ((f32[64,1,576]{2,1,0:T(1,128)}), f32[64,1,576]{2,1,0:T(1,128)S(1)}, u32[]{:S(2)}, u32[]{:S(2)}) async-start(f32[64,1,576]{2,1,0:T(1,128)} %reshape.22), calls=%async_computation | async-start | bytes 327680 | tf_op jit(solution)/shard_map/all_to_all | solution.py:38
  32.3 132.7 %all-reduce.5.cloned.1.call-start = ((), (), s32[]{:S(2)}) async-start(), calls=%async_computation.3 | async-start | bytes 786432 | tf_op jit(solution)/shard_map/psum | solution.py:41
  51.7 1.3 copy-start.1
  51.7 1.5 copy-start.2
  52.5 573.3 %all-reduce.3.cloned.1.call-start = ((), (), s32[]{:S(2)}) async-start(), calls=%async_computation.2 | async-start | bytes 393216 | tf_op jit(solution)/shard_map/psum | solution.py:40
  54.5 0.9 copy-start.5
  55.4 0.7 copy-start.6
  55.4 0.7 copy-start.7
  56.1 27.7 %copy-start.8 = (f32[4,12]{1,0:T(4,128)S(1)}, f32[4,12]{1,0:T(4,128)}, u32[]{:S(2)}) copy-start(f32[4,12]{1,0:T(4,128)} %param.19) | copy-start | bytes 580
  166.1 459.7 %copy-start.3 = (f32[240,768]{1,0:T(8,128)S(1)}, f32[240,768]{1,0:T(8,128)}, u32[]{:S(2)}) copy-start(f32[240,768]{1,0:T(8,128)} %param.12) | copy-start | bytes 2211844
  167.1 463.2 %all-to-all-start.1 = ((bf16[64,2,288]{2,1,0:T(2,128)(2,1)}), bf16[64,2,288]{2,1,0:T(2,128)(2,1)S(1)}, u32[]{:S(2)}, u32[]{:S(2)}) async-start(bf16[64,2,288]{2,1,0:T(2,128)(2,1)} %reshape.24), calls=%async_computation.1 | async-start | bytes 196608 | tf_op jit(solution)/shard_map/all_to_all | solution.py:51
Sparse Core Ops, SparseCore 0:
  52.7 112.3 all-reduce.4
  171.9 453.8 all-reduce.2
where the time goes:
time: 639 us; the launch traced here: 638 us
  waiting for transfers between devices  540 us (85%)
  starting transfers between devices  38.6 us (6%)
  blocking collectives  27.7 us (4%)
  between operations  14.2 us (2%)
  local copies, waits for them, and re-layouts  8.4 us (1%)
    psum x1, waiting for transfers between devices, on_device(): coeff_sum = lax.psum(partial_coeff, ('group', 'shard'))  442 us
    psum x1, waiting for transfers between devices, on_device(): attn_sum, norm_sum = lax.psum((attn_term, norm_diff), 'group')  80.6 us
    psum x1, blocking collectives, on_device(): attn_sum, norm_sum = lax.psum((attn_term, norm_diff), 'group')  27.7 us
    all_to_all x1, starting transfers between devices, on_device(): lax.all_to_all(inner_attn[0], 'shard', split_axis=1, concat_axis=0, tiled...  22.4 us
    all_to_all x1, waiting for transfers between devices, on_device(): lax.all_to_all(inner_attn[0], 'shard', split_axis=1, concat_axis=0, tiled...  17.3 us
    all_to_all x1, starting transfers between devices, on_device(): lax.all_to_all(new_attn.astype(jnp.bfloat16), 'shard', split_axis=0, conc...  16.1 us
  transfers between devices with their start and end apart: 4, of which 3 were waited for; matrix products, arithmetic and copies ran while one was open for 1% of the time, Pallas kernels for 0%

commit v1 on v0

--- a/solution.py
+++ b/solution.py
@@ -35,7 +35,12 @@
         preferred_element_type=jnp.float32,
     )
     norm_diff = outer_norms - inner_norms[0]
-    moved = lax.all_to_all(inner_attn[0], "shard", split_axis=1, concat_axis=0, tiled=True)
+    moved = jnp.concatenate(
+        lax.all_to_all(
+            jnp.stack(jnp.split(inner_attn[0], lax.axis_size("shard"), axis=1)), "shard", 0, 0
+        ),
+        axis=0,
+    )
     attn_term = outer_attn - moved
     coeff_sum = lax.psum(partial_coeff, ("group", "shard"))
     attn_sum, norm_sum = lax.psum((attn_term, norm_diff), "group")

time: 639 us -> 653 us (1.022)
  waiting for transfers between devices: 540 us -> 548 us
    psum x1, waiting for transfers between devices: 442 us -> 452 us  [on_device(): coeff_sum = lax.psum(partial_coeff, ('group', 'shard'))]
where the time goes in v1:
time: 653 us; the launch traced here: 651 us
  waiting for transfers between devices  548 us (84%)
  starting transfers between devices  38.6 us (6%)
  blocking collectives  28.5 us (4%)
  between operations  14.2 us (2%)
  local copies, waits for them, and re-layouts  13.1 us (2%)
    psum x1, waiting for transfers between devices, on_device(): coeff_sum = lax.psum(partial_coeff, ('group', 'shard'))  452 us
    psum x1, waiting for transfers between devices, on_device(): attn_sum, norm_sum = lax.psum((attn_term, norm_diff), 'group')  79.1 us
    psum x1, blocking collectives, on_device(): attn_sum, norm_sum = lax.psum((attn_term, norm_diff), 'group')  28.5 us
    all_to_all x1, starting transfers between devices, on_device(): lax.all_to_all(jnp.stack(jnp.split(inner_attn[0], lax.axis_size('shard'),...  22.4 us
    all_to_all x1, waiting for transfers between devices, on_device(): lax.all_to_all(jnp.stack(jnp.split(inner_attn[0], lax.axis_size('shard'),...  17.3 us
    all_to_all x1, starting transfers between devices, on_device(): lax.all_to_all(new_attn.astype(jnp.bfloat16), 'shard', split_axis=0, conc...  16.1 us
  transfers between devices with their start and end apart: 4, of which 3 were waited for; matrix products, arithmetic and copies ran while one was open for 1% of the time, Pallas kernels for 0%

profile of v1, /device:TPU:1, one launch (start us, length us, event | category | flops | bytes accessed | tf_op | source)
XLA Modules:
  0.0 651.3 jit_solution(12243828588606453239)
XLA Ops:
  7.2 1.0 copy.27
  8.2 0.1 constant_dynamic-update-slice_fusion.62
  11.2 0.1 constant_dynamic-update-slice_fusion.14
  11.3 0.1 constant_dynamic-update-slice_fusion.13
  11.8 0.1 constant_dynamic-update-slice_fusion.6
  11.8 0.1 constant_dynamic-update-slice_fusion.5
  12.3 1.1 reshape.21
  13.4 22.4 %all-to-all-start = ((f32[64,1,576]{2,1,0:T(1,128)}), f32[64,1,576]{2,1,0:T(1,128)S(1)}, u32[]{:S(2)}, u32[]{:S(2)}) async-start(f32[64,1,576]{2,1,0:T(1,128)} %reshape.21), calls=%async_computation | async-start | bytes 327680 | tf_op jit(solution)/shard_map/all_to_all | solution.py:39
  35.8 0.2 copy.21
  36.0 17.3 %all-to-all-done = f32[64,1,576]{2,1,0:T(1,128)S(1)} async-done(((f32[64,1,576]{2,1,0:T(1,128)}), f32[64,1,576]{2,1,0:T(1,128)S(1)}, u32[]{:S(2)}, u32[]{:S(2)}) %all-to-all-start) | async-done | bytes 147488 | tf_op jit(solution)/shard_map/all_to_all | solution.py:39
  53.3 0.5 broadcast.28
  53.8 1.0 reduce
  54.8 0.2 reshape.22
  55.1 0.8 sub.20
  56.0 0.4 copy-done.1
  56.4 0.2 copy-done.3
  56.6 2.2 convolution_bitcast_fusion
  58.8 0.9 copy-done.5
  59.7 0.2 copy.20
  59.8 0.5 copy-done.6
  60.4 28.5 %psum.23 = f32[4,12]{1,0:T(4,128)S(1)} all-reduce(f32[4,12]{1,0:T(4,128)S(1)} %bitcast_subtract_fusion.2), channel_id=1, replica_groups=mesh['group'=8,'shard'=64] {'group'}, use_global_device_ids=true, to_apply=%region_2.0 | all-reduce | flops 48 | bytes 384 | tf_op jit(solution)/shard_map/psum | solution.py:46
  88.8 0.6 add_subtract_fusion.2
  89.4 79.1 %all-reduce.5.cloned.1.call-done = f32[768,48]{1,0:T(8,128)} async-done(((f32[768,48]{1,0:T(8,128)}), f32[768,48]{1,0:T(8,128)}) %all-reduce.5.cloned.1.call-update) | async-done | bytes 147472 | tf_op jit(solution)/shard_map/psum | solution.py:46
  168.5 1.1 fusion.4
  169.7 0.9 reshape.23
  170.6 16.1 %all-to-all-start.1 = ((bf16[64,2,288]{2,1,0:T(2,128)(2,1)}), bf16[64,2,288]{2,1,0:T(2,128)(2,1)S(1)}, u32[]{:S(2)}, u32[]{:S(2)}) async-start(bf16[64,2,288]{2,1,0:T(2,128)(2,1)} %reshape.23), calls=%async_computation.1 | async-start | bytes 196608 | tf_op jit(solution)/shard_map/all_to_all | solution.py:56
  186.8 451.9 %all-reduce.3.cloned.1.call-done = f32[64,768]{0,1:T(8,128)} async-done(((f32[64,768]{0,1:T(8,128)}), f32[64,768]{0,1:T(8,128)}) %all-reduce.3.cloned.1.call-update) | async-done | bytes 196624 | tf_op jit(solution)/shard_map/psum | solution.py:45
  638.7 3.0 add_subtract_fusion
  641.7 0.8 copy.23
  642.5 0.8 copy.24
  643.3 0.2 reshape.24
  643.6 0.9 all_to_all.21
  (82 shorter events, 4.0 us)
Async XLA Ops:
  7.2 48.8 %copy-start = (f32[240,64]{0,1:T(8,128)S(1)}, f32[240,64]{0,1:T(8,128)}, u32[]{:S(2)}) copy-start(f32[240,64]{0,1:T(8,128)} %param.13) | copy-start | bytes 184324
  13.4 22.4 %copy-start.4 = (f32[768,48]{0,1:T(8,128)S(1)}, f32[768,48]{0,1:T(8,128)}, u32[]{:S(2)}) copy-start(f32[768,48]{0,1:T(8,128)} %param.15) | copy-start | bytes 442372
  13.4 39.9 %all-to-all-start = ((f32[64,1,576]{2,1,0:T(1,128)}), f32[64,1,576]{2,1,0:T(1,128)S(1)}, u32[]{:S(2)}, u32[]{:S(2)}) async-start(f32[64,1,576]{2,1,0:T(1,128)} %reshape.21), calls=%async_computation | async-start | bytes 327680 | tf_op jit(solution)/shard_map/all_to_all | solution.py:39
  35.8 132.7 %all-reduce.5.cloned.1.call-start = ((), (), s32[]{:S(2)}) async-start(), calls=%async_computation.3 | async-start | bytes 786432 | tf_op jit(solution)/shard_map/psum | solution.py:46
  55.1 1.3 copy-start.1
  55.1 1.5 copy-start.3
  55.9 582.8 %all-reduce.3.cloned.1.call-start = ((), (), s32[]{:S(2)}) async-start(), calls=%async_computation.2 | async-start | bytes 786432 | tf_op jit(solution)/shard_map/psum | solution.py:45
  58.7 0.9 copy-start.5
  59.6 0.7 copy-start.6
  59.7 0.7 copy-start.7
  60.4 28.5 %copy-start.8 = (f32[4,12]{1,0:T(4,128)S(1)}, f32[4,12]{1,0:T(4,128)}, u32[]{:S(2)}) copy-start(f32[4,12]{1,0:T(4,128)} %param.19) | copy-start | bytes 580
  169.6 469.1 %copy-start.2 = (f32[240,768]{1,0:T(8,128)S(1)}, f32[240,768]{1,0:T(8,128)}, u32[]{:S(2)}) copy-start(f32[240,768]{1,0:T(8,128)} %param.12) | copy-start | bytes 2211844
  170.6 472.7 %all-to-all-start.1 = ((bf16[64,2,288]{2,1,0:T(2,128)(2,1)}), bf16[64,2,288]{2,1,0:T(2,128)(2,1)S(1)}, u32[]{:S(2)}, u32[]{:S(2)}) async-start(bf16[64,2,288]{2,1,0:T(2,128)(2,1)} %reshape.23), calls=%async_computation.1 | async-start | bytes 196608 | tf_op jit(solution)/shard_map/all_to_all | solution.py:56
Sparse Core Ops, SparseCore 0:
  56.0 112.4 all-reduce.4
  175.3 463.3 all-reduce.2

commit v2 on v0

--- a/solution.py
+++ b/solution.py
@@ -37,7 +37,7 @@
     norm_diff = outer_norms - inner_norms[0]
     moved = lax.all_to_all(inner_attn[0], "shard", split_axis=1, concat_axis=0, tiled=True)
     attn_term = outer_attn - moved
-    coeff_sum = lax.psum(partial_coeff, ("group", "shard"))
+    coeff_sum = lax.psum(lax.psum(partial_coeff, "group"), "shard")
     attn_sum, norm_sum = lax.psum((attn_term, norm_diff), "group")
     attn_delta = attn_sum / groups
     norm_delta = norm_sum / groups

time: 639 us -> 1200 us (1.88)
  waiting for transfers between devices: 540 us -> 1100 us
    psum x2, waiting for transfers between devices: 523 us -> 1090 us  [on_device(): coeff_sum = lax.psum(lax.psum(partial_coeff, 'group'), 'shard')]
where the time goes in v2:
time: 1200 us
  waiting for transfers between devices  1100 us (92%)
  starting transfers between devices  38.3 us (3%)
  blocking collectives  27.9 us (2%)
  between operations  14.2 us (1%)
    psum x2, waiting for transfers between devices, on_device(): coeff_sum = lax.psum(lax.psum(partial_coeff, 'group'), 'shard')  1090 us
    psum x1, blocking collectives, on_device(): attn_sum, norm_sum = lax.psum((attn_term, norm_diff), 'group')  27.9 us
  transfers between devices with their start and end apart: 4, of which 3 were waited for; matrix products, arithmetic and copies ran while one was open for 1% of the time, Pallas kernels for 0%

profile of v2, /device:TPU:1, one launch (start us, length us, event | category | flops | bytes accessed | tf_op | source)
XLA Modules:
  0.0 1200.6 jit_solution(12373521406950182621)
XLA Ops:
  7.2 1.3 reduce
  8.5 0.2 all_to_all.28
  8.7 0.2 copy.34
  8.9 1.0 reshape.22
  10.0 22.4 %all-to-all-start = ((f32[64,1,576]{2,1,0:T(1,128)}), f32[64,1,576]{2,1,0:T(1,128)S(1)}, u32[]{:S(2)}, u32[]{:S(2)}) async-start(f32[64,1,576]{2,1,0:T(1,128)} %reshape.22), calls=%async_computation | async-start | bytes 327680 | tf_op jit(solution)/shard_map/all_to_all | solution.py:38
  32.4 0.0 all-reduce.6.cloned.1.call-start
  32.4 0.2 copy.29
  32.6 0.2 copy.28
  32.8 1.3 convolution_bitcast_fusion
  34.1 15.8 %all-to-all-done = f32[64,1,576]{2,1,0:T(1,128)S(1)} async-done(((f32[64,1,576]{2,1,0:T(1,128)}), f32[64,1,576]{2,1,0:T(1,128)S(1)}, u32[]{:S(2)}, u32[]{:S(2)}) %all-to-all-start) | async-done | bytes 147488 | tf_op jit(solution)/shard_map/all_to_all | solution.py:38
  49.9 0.5 broadcast.29
  50.4 1.0 reduce.1
  51.4 0.2 reshape.23
  51.7 0.8 sub.20
  52.5 0.0 all-reduce.6.cloned.1.call-update
  52.5 0.0 all-reduce.4.cloned.1.call-start
  52.6 0.6 copy-done.6
  53.2 27.9 %psum.31 = f32[4,12]{1,0:T(4,128)S(1)} all-reduce(f32[4,12]{1,0:T(4,128)S(1)} %bitcast_subtract_fusion.2), channel_id=1, replica_groups=mesh['group'=8,'shard'=64] {'group'}, use_global_device_ids=true, to_apply=%region_3.0 | all-reduce | flops 48 | bytes 384 | tf_op jit(solution)/shard_map/psum | solution.py:41
  81.2 0.6 add_subtract_fusion.2
  81.7 85.4 %all-reduce.6.cloned.1.call-done = (f32[64,768]{1,0:T(8,128)}, f32[768,48]{1,0:T(8,128)}) async-done(((f32[64,768]{1,0:T(8,128)}, f32[768,48]{1,0:T(8,128)}), (f32[64,768]{1,0:T(8,128)}, f32[768,48]{1,0:T(8,128)})) %all-reduce.6.cloned.1.call-update) | async-done | bytes 344080 | tf_op jit(solution)/shard_map/psum | solution.py:40
  167.2 0.0 all-reduce.4.cloned.1.call-update
  167.2 1.1 fusion.4
  168.3 0.1 all_to_all.32
  168.4 0.9 reshape.24
  169.3 15.8 %all-to-all-start.1 = ((bf16[64,2,288]{2,1,0:T(2,128)(2,1)}), bf16[64,2,288]{2,1,0:T(2,128)(2,1)S(1)}, u32[]{:S(2)}, u32[]{:S(2)}) async-start(bf16[64,2,288]{2,1,0:T(2,128)(2,1)} %reshape.24), calls=%async_computation.1 | async-start | bytes 196608 | tf_op jit(solution)/shard_map/all_to_all | solution.py:51
  185.2 0.8 copy.31
  186.0 0.8 copy.32
  186.8 1002.8 %all-reduce.4.cloned.1.call-done = f32[64,768]{1,0:T(8,128)} async-done(((f32[64,768]{1,0:T(8,128)}), f32[64,768]{1,0:T(8,128)}) %all-reduce.4.cloned.1.call-update) | async-done | bytes 196624 | tf_op jit(solution)/shard_map/psum | solution.py:40
  1189.6 2.9 add_subtract_fusion
  1192.5 0.2 reshape.25
  1192.7 0.1 copy.30
  1192.8 0.9 all_to_all.35
  (21 shorter events, 0.1 us)
Async XLA Ops:
  7.2 25.6 %copy-start = (f32[240,64]{0,1:T(8,128)S(1)}, f32[240,64]{0,1:T(8,128)}, u32[]{:S(2)}) copy-start(f32[240,64]{0,1:T(8,128)} %param.13) | copy-start | bytes 184324
  8.9 23.5 %copy-start.4 = (f32[768,48]{0,1:T(8,128)S(1)}, f32[768,48]{0,1:T(8,128)}, u32[]{:S(2)}) copy-start(f32[768,48]{0,1:T(8,128)} %param.15) | copy-start | bytes 442372
  8.9 23.7 %copy-start.5 = (f32[768,48]{0,1:T(8,128)S(1)}, f32[768,48]{0,1:T(8,128)}, u32[]{:S(2)}) copy-start(f32[768,48]{0,1:T(8,128)} %param.16) | copy-start | bytes 442372
  8.9 23.8 %copy-start.2 = (f32[1,240,768]{2,1,0:T(8,128)S(1)}, f32[1,240,768]{2,1,0:T(8,128)}, u32[]{:S(2)}) copy-start(f32[1,240,768]{2,1,0:T(8,128)} %param.10) | copy-start | bytes 2211844
  10.0 22.8 %copy-start.1 = (f32[240,768]{1,0:T(8,128)S(1)}, f32[240,768]{1,0:T(8,128)}, u32[]{:S(2)}) copy-start(f32[240,768]{1,0:T(8,128)} %param.11) | copy-start | bytes 2211844
  10.0 39.9 %all-to-all-start = ((f32[64,1,576]{2,1,0:T(1,128)}), f32[64,1,576]{2,1,0:T(1,128)S(1)}, u32[]{:S(2)}, u32[]{:S(2)}) async-start(f32[64,1,576]{2,1,0:T(1,128)} %reshape.22), calls=%async_computation | async-start | bytes 327680 | tf_op jit(solution)/shard_map/all_to_all | solution.py:38
  32.4 134.8 %all-reduce.6.cloned.1.call-start = ((), (), s32[]{:S(2)}) async-start(), calls=%async_computation.3 | async-start | bytes 1179648 | tf_op jit(solution)/shard_map/psum | solution.py:40
  52.5 0.7 copy-start.6
  52.5 0.7 copy-start.7
  52.5 1137.0 %all-reduce.4.cloned.1.call-start = ((), (), s32[]{:S(2)}) async-start(), calls=%async_computation.2 | async-start | bytes 393216 | tf_op jit(solution)/shard_map/psum | solution.py:40
  53.2 27.9 %copy-start.8 = (f32[4,12]{1,0:T(4,128)S(1)}, f32[4,12]{1,0:T(4,128)}, u32[]{:S(2)}) copy-start(f32[4,12]{1,0:T(4,128)} %param.19) | copy-start | bytes 580
  168.4 1021.2 %copy-start.3 = (f32[240,768]{1,0:T(8,128)S(1)}, f32[240,768]{1,0:T(8,128)}, u32[]{:S(2)}) copy-start(f32[240,768]{1,0:T(8,128)} %param.12) | copy-start | bytes 2211844
  169.3 1023.2 %all-to-all-start.1 = ((bf16[64,2,288]{2,1,0:T(2,128)(2,1)}), bf16[64,2,288]{2,1,0:T(2,128)(2,1)S(1)}, u32[]{:S(2)}, u32[]{:S(2)}) async-start(bf16[64,2,288]{2,1,0:T(2,128)(2,1)} %reshape.24), calls=%async_computation.1 | async-start | bytes 196608 | tf_op jit(solution)/shard_map/all_to_all | solution.py:51
Sparse Core Ops, SparseCore 0:
  52.7 114.4 all-reduce.5
  170.1 1019.4 all-reduce.3
